TPU v7x, 32 devices: a whole 2x2x4 slice. The times are simulated.
32 devices in a mesh: group: 2 (over y), shard: 16 (over z, x, core).
Axes of the slice: x: 2, y: 2, z: 4, core: 2. Of those that a mesh axis runs over, the one named last changes fastest.
Arguments:
- samples: bfloat16 [32, 8192], P('shard'), may hold values from -6 to 6
- factor_old: float32 [8192, 8192], P('shard', 'group'), as said below
- damping: float32 [1], replicated, may hold values from 0.1 to 1
- gradients: bfloat16 [2048, 8192], P('shard', 'group'), may hold values from -6 to 6
Outputs:
- swept_factor: float32 [8192, 8192], P('shard', 'group')
- update: bfloat16 [8192, 2048], P('shard', 'group')
Inputs may be any that keep to these rules, and one draw needn't show every extreme that they name: factor_old is symmetric and positive definite.
All inputs are finite; a program needn't handle non-finite values.
Results may differ from a plain program's by a relative error of at most 0.0049.
Values may be sent and summed in bfloat16 or wider, within the bound.
A program may use at most 128 MiB of HBM per device.

v0:
```python
import jax
import jax.numpy as jnp
from jax import lax
from jax.sharding import PartitionSpec as P

D = 8192
BLOCK = 128
PIVOTS = 2
ema_keep = 0.5


def spread(block, axis, holder):
    block = jnp.where(lax.axis_index(axis) == holder, block, jnp.zeros_like(block))
    return lax.psum(block, axis)


def solve_spd(pivot_block, right_side):
    lower_factor = jnp.linalg.cholesky(pivot_block)
    half_solved = lax.linalg.triangular_solve(lower_factor, right_side, left_side=True, lower=True)
    return lax.linalg.triangular_solve(
        lower_factor, half_solved, left_side=True, lower=True, transpose_a=True
    )


def on_device(samples, factor_old, damping, gradients):
    row_count, col_count = factor_old.shape
    shard_index = lax.axis_index("shard")
    group_index = lax.axis_index("group")
    row_first = shard_index * row_count
    col_first = group_index * col_count
    total_tokens = samples.shape[0] * lax.axis_size("shard")
    contract = (((0,), (0,)), ((), ()))
    token_piece = lax.all_gather(samples, "shard", axis=0, tiled=True)
    left_part = lax.dynamic_slice_in_dim(token_piece, row_first, row_count, 1)
    right_part = lax.dynamic_slice_in_dim(token_piece, col_first, col_count, 1)
    covariance = lax.dot_general(
        left_part, right_part, contract, preferred_element_type=jnp.float32
    )
    row_ids = lax.broadcasted_iota(jnp.int32, (row_count, col_count), 0) + row_first
    col_ids = lax.broadcasted_iota(jnp.int32, (row_count, col_count), 1) + col_first
    diagonal = jnp.where(row_ids == col_ids, damping[0], 0.0)
    factor = ema_keep * factor_old + (1.0 - ema_keep) * (covariance / total_tokens) + diagonal
    spacing = D // PIVOTS
    sel_rows = lax.broadcasted_iota(jnp.int32, (BLOCK, col_count), 0)
    sel_cols = lax.broadcasted_iota(jnp.int32, (BLOCK, col_count), 1) + col_first

    def sweep_once(sweep_step, matrix):
        first_index = (sweep_step * spacing).astype(jnp.int32)
        col_owner = first_index // col_count
        row_owner = first_index // row_count
        col_offset = first_index - col_owner * col_count
        row_offset = first_index - row_owner * row_count
        own_columns = lax.dynamic_slice_in_dim(matrix, col_offset, BLOCK, 1)
        column = spread(own_columns, "group", col_owner)
        own_rows = lax.dynamic_slice_in_dim(matrix, row_offset, BLOCK, 0)
        own_pivot = lax.dynamic_slice_in_dim(column, row_offset, BLOCK, 0)
        pivot_strip, pivot_block = (
            spread(own_rows, "shard", row_owner),
            spread(own_pivot, "shard", row_owner),
        )
        selector = jnp.where(sel_cols == sel_rows + first_index, 1.0, 0.0).astype(jnp.float32)
        factor_q = solve_spd(pivot_block, pivot_strip + selector)
        matrix = matrix - jnp.dot(
            column, factor_q, precision=lax.Precision.HIGHEST, preferred_element_type=jnp.float32
        )
        addition = jnp.where(shard_index == row_owner, factor_q, 0.0)
        block_rows = lax.dynamic_slice_in_dim(matrix, row_offset, BLOCK, 0) + addition
        return lax.dynamic_update_slice_in_dim(matrix, block_rows, row_offset, 0)

    swept_factor = lax.fori_loop(0, PIVOTS, sweep_once, factor)
    swept_half = swept_factor.astype(jnp.bfloat16)
    partial_terms = lax.dot_general(
        swept_half,
        lax.all_gather(gradients, "shard", axis=0, tiled=True),
        (((1,), (1,)), ((), ())),
        preferred_element_type=jnp.float32,
    )
    update = lax.psum_scatter(partial_terms, "group", scatter_dimension=1, tiled=True).astype(
        jnp.bfloat16
    )
    return (swept_factor, update)


def solution(mesh):
    return jax.shard_map(
        on_device,
        mesh=mesh,
        in_specs=(P("shard", None), P("shard", "group"), P(), P("shard", "group")),
        out_specs=(P("shard", "group"), P("shard", "group")),
        check_vma=False,
    )
```

profile of v0, /device:TPU:0, one launch (start us, length us, event | category | flops | bytes accessed | tf_op | source)
XLA Modules:
  0.0 591.6 jit_solution(10280611587841758913)
XLA Ops:
  8.0 24.8 %all-gather = bf16[16,2,8192]{2,1,0:T(2,128)(2,1)S(1)} all-gather(bf16[1,2,8192]{2,1,0:T(2,128)(2,1)} %bitcast.32), channel_id=1, replica_groups=mesh['group'=2,'shard'=16] {'shard'}, dimensions={0}, use_global_device_ids=true | all-gather | bytes 557056 | tf_op jit(solution)/shard_map/all_gather | solution.py:33
  33.7 6.7 %select_add_fusion = f32[512,4096]{1,0:T(8,128)} fusion(f32[512,4096]{1,0:T(8,128)} %param.7, f32[]{:T(128)} %bitcast.31, s32[4096]{0:T(1024)S(1)} %iota_add_fusion.1, s32[512]{0:T(512)S(1)} %iota_add_fusion.2, bf16[32,8192]{1,0:T(8,128)(2,1)S(1)} %reshape.41, s32[]{:T(128)S(6)} %select_n.180, s32[]{:T(128)S(6)} %select_n.179), kind=kOutput, calls=%fused_computation.29 | convolution fusion | flops 146800640 | bytes 17090572 | tf_op jit(solution)/shard_map/dot_general | solution.py:36
  40.4 345.1 %while.17 = (s32[]{:T(128)}, f32[512,4096]{1,0:T(8,128)}, s32[]{:T(128)}, s32[4096]{0:T(1024)S(1)}, s32[]{:T(128)}, /*index=5*/s32[]{:T(128)}, s32[]{:T(128)}, s...) while((s32[]{:T(128)}, f32[512,4096]{1,0:T(8,128)}, ...), condition=%wide.region_6.7_spmd.clone, body=%wide.region_0.6_spmd.clone.sunk | while | flops 4838440960 | bytes 54937316 | solution.py:70
  42.2 3.1 dynamic-slice_select_fusion.7
  45.3 19.4 %all-reduce.6.cloned.1.call-done = f32[512,128]{1,0:T(8,128)} async-done(((f32[512,128]{1,0:T(8,128)}), f32[512,128]{1,0:T(8,128)}) %all-reduce.6.cloned.1.call-update) | async-done | bytes 262160 | tf_op jit(solution)/shard_map/while/body/eval_jaxpr/psum | solution.py:14
  66.1 101.6 %all-reduce.8.cloned.1.call-done = (f32[128,4096]{1,0:T(8,128)}, f32[128,128]{1,0:T(8,128)}) async-done(((f32[128,4096]{1,0:T(8,128)}, f32[128,128]{1,0:T(8,128)}), (f32[128,4096]{1,0:T(8,128)}, f32[128,128]{1,0:T(8,128)})) %all-reduce.8.cloned.1.call-update) | async-done | bytes 2162704 | tf_op jit(solution)/shard_map/while/body/eval_jaxpr/psum | solution.py:14
  169.5 11.7 %cholesky.59 = f32[128,128]{1,0:T(8,128)S(1)} custom-call(f32[128,128]{1,0:T(8,128)S(1)} %fusion.45), custom_call_target="Cholesky" | custom-call | tf_op jit(solution)/shard_map/while/body/eval_jaxpr/jit(cholesky)/cholesky | solution.py:18
  182.6 9.8 %custom-call.26 = f32[1,128,128]{1,2,0:T(8,128)S(1)} custom-call(f32[1,128,128]{2,1,0:T(8,128)S(1)} %fusion.46), custom_call_target="InvertDiagBlocksLowerTriangular" | custom-call | tf_op jit(solution)/shard_map/while/body/eval_jaxpr/triangular_solve | solution.py:20
  192.4 3.6 fusion.47
  196.0 1.9 fusion.48
  197.9 11.1 %convolution_subtract_fusion.2 = f32[512,4096]{1,0:T(8,128)} fusion(f32[512,4096]{1,0:T(8,128)} %get-tuple-element.225, f32[512,128]{1,0:T(8,128)S(1)} %copy-done, f32[128,4096]{1,0:T(8,128)S(1)} %fusion.48), kind=kOutput, calls=%fused_computation.2.clone.1 | convolution fusion | flops 3223322624 | bytes 19136512 | tf_op jit(solution)/shard_map/while/body/eval_jaxpr/dot_general | solution.py:63
  209.1 3.2 add_dynamic-update-slice_fusion.2
  214.1 3.1 dynamic-slice_select_fusion.7
  217.2 20.8 %all-reduce.6.cloned.1.call-done = f32[512,128]{1,0:T(8,128)} async-done(((f32[512,128]{1,0:T(8,128)}), f32[512,128]{1,0:T(8,128)}) %all-reduce.6.cloned.1.call-update) | async-done | bytes 262160 | tf_op jit(solution)/shard_map/while/body/eval_jaxpr/psum | solution.py:14
  239.4 101.5 %all-reduce.8.cloned.1.call-done = (f32[128,4096]{1,0:T(8,128)}, f32[128,128]{1,0:T(8,128)}) async-done(((f32[128,4096]{1,0:T(8,128)}, f32[128,128]{1,0:T(8,128)}), (f32[128,4096]{1,0:T(8,128)}, f32[128,128]{1,0:T(8,128)})) %all-reduce.8.cloned.1.call-update) | async-done | bytes 2162704 | tf_op jit(solution)/shard_map/while/body/eval_jaxpr/psum | solution.py:14
  342.7 11.7 %cholesky.59 = f32[128,128]{1,0:T(8,128)S(1)} custom-call(f32[128,128]{1,0:T(8,128)S(1)} %fusion.45), custom_call_target="Cholesky" | custom-call | tf_op jit(solution)/shard_map/while/body/eval_jaxpr/jit(cholesky)/cholesky | solution.py:18
  355.7 9.8 %custom-call.26 = f32[1,128,128]{1,2,0:T(8,128)S(1)} custom-call(f32[1,128,128]{2,1,0:T(8,128)S(1)} %fusion.46), custom_call_target="InvertDiagBlocksLowerTriangular" | custom-call | tf_op jit(solution)/shard_map/while/body/eval_jaxpr/triangular_solve | solution.py:20
  365.6 3.6 fusion.47
  371.1 11.1 %convolution_subtract_fusion.2 = f32[512,4096]{1,0:T(8,128)} fusion(f32[512,4096]{1,0:T(8,128)} %get-tuple-element.225, f32[512,128]{1,0:T(8,128)S(1)} %copy-done, f32[128,4096]{1,0:T(8,128)S(1)} %fusion.48), kind=kOutput, calls=%fused_computation.2.clone.1 | convolution fusion | flops 3223322624 | bytes 19136512 | tf_op jit(solution)/shard_map/while/body/eval_jaxpr/dot_general | solution.py:63
  382.2 3.2 add_dynamic-update-slice_fusion.2
  386.1 126.8 %all-gather.3.cloned.1.call-done = bf16[2048,4096]{1,0:T(8,128)(2,1)} async-done(((bf16[128,4096]{1,0:T(8,128)(2,1)}), bf16[2048,4096]{1,0:T(8,128)(2,1)}) %all-gather.3.cloned.1.call-update) | async-done | bytes 16777232 | tf_op jit(solution)/shard_map/all_gather | solution.py:74
  512.9 16.2 %fusion.20 = f32[512,2048]{1,0:T(8,128)} fusion(bf16[2048,4096]{1,0:T(8,128)(2,1)} %all-gather.3.cloned.1.call-done, f32[512,4096]{1,0:T(8,128)} %get-tuple-element.154), kind=kOutput, calls=%fused_computation.30 | convolution fusion | flops 8592031744 | bytes 29360128 | tf_op jit(solution)/shard_map/dot_general | solution.py:72
  529.1 52.6 %reduce-scatter.2.cloned.1.call-done = f32[512,1024]{1,0:T(8,128)} async-done(((f32[512,2048]{1,0:T(8,128)}), f32[512,1024]{1,0:T(8,128)}) %reduce-scatter.2.cloned.1.call-update) | async-done | bytes 2097168 | tf_op jit(solution)/shard_map/reduce_scatter | solution.py:78
  581.7 2.7 convert_element_type.7
  (34 shorter events, 15.4 us)
Async XLA Ops:
  40.4 24.2 %all-reduce.6.cloned.1.call-start = ((), (), s32[]{:S(2)}) async-start(), calls=%async_computation.3 | async-start | bytes 524288 | tf_op jit(solution)/shard_map/while/body/eval_jaxpr/psum | solution.py:14
  42.1 125.6 %all-reduce.8.cloned.1.call-start = ((), (), s32[]{:S(2)}) async-start(), calls=%async_computation.4 | async-start | bytes 4325376 | tf_op jit(solution)/shard_map/while/body/eval_jaxpr/psum | solution.py:14
  192.4 5.6 copy-start
  212.3 25.6 %all-reduce.6.cloned.1.call-start = ((), (), s32[]{:S(2)}) async-start(), calls=%async_computation.3 | async-start | bytes 524288 | tf_op jit(solution)/shard_map/while/body/eval_jaxpr/psum | solution.py:14
  214.0 126.9 %all-reduce.8.cloned.1.call-start = ((), (), s32[]{:S(2)}) async-start(), calls=%async_computation.4 | async-start | bytes 4325376 | tf_op jit(solution)/shard_map/while/body/eval_jaxpr/psum | solution.py:14
  365.6 5.6 copy-start
  385.5 127.5 %all-gather.3.cloned.1.call-start = ((), (), s32[]{:S(2)}) async-start(), calls=%async_computation.1 | async-start | bytes 17825792 | tf_op jit(solution)/shard_map/all_gather | solution.py:74
  386.0 195.7 %reduce-scatter.2.cloned.1.call-start = ((), (), s32[]{:S(2)}) async-start(), calls=%async_computation.2 | async-start | bytes 6291456 | tf_op jit(solution)/shard_map/reduce_scatter | solution.py:78
Sparse Core Ops, SparseCore 0:
  44.0 20.5 all-reduce.5
  68.8 98.8 all-reduce.7
  215.9 21.9 all-reduce.5
  241.9 98.9 all-reduce.7
Sparse Core Ops, SparseCore 1:
  388.1 124.8 all-gather.2
  529.2 52.5 reduce-scatter.1
where the time goes:
time: 592 us
  waiting for transfers between devices  423 us (71%)
  other arithmetic  69.1 us (12%)
  matrix products  56.1 us (9%)
  blocking collectives  24.8 us (4%)
  between operations  15.8 us (3%)
    psum x4, waiting for transfers between devices, spread(): return lax.psum(block, axis)  243 us
    all_gather x1, waiting for transfers between devices, on_device(): lax.all_gather(gradients, 'shard', axis=0, tiled=True)  127 us
    reduce_scatter x1, waiting for transfers between devices, on_device(): lax.psum_scatter(partial_terms, 'group', scatter_dimension=1, tiled=True)  52.6 us
    all_gather x1, blocking collectives, on_device(): token_piece = lax.all_gather(samples, 'shard', axis=0, tiled=True)  24.8 us
    another operation x6, other arithmetic, solve_spd(): lower_factor = jnp.linalg.cholesky(pivot_block)  24.8 us
    dot_general x2, matrix products, sweep_once(): jnp.dot(column, factor_q, precision=lax.Precision.HIGHEST, preferred_elem...  22.2 us
    another operation x4, other arithmetic, solve_spd(): lax.linalg.triangular_solve(lower_factor, half_solved, left_side=True, lo...  20.9 us
    dot_general x1, matrix products, on_device(): lax.dot_general(swept_half, lax.all_gather(gradients, 'shard', axis=0, ti...  16.2 us
  transfers between devices with their start and end apart: 6, of which 6 were waited for; matrix products, arithmetic and copies ran while one was open for 1% of the time, Pallas kernels for 0%

commit v1 on v0

--- a/solution.py
+++ b/solution.py
@@ -7,6 +7,18 @@
 BLOCK = 128
 PIVOTS = 2
 ema_keep = 0.5
+
+
+def doubled_up(shard, axis, dim):
+    ways, here = (lax.axis_size(axis), lax.axis_index(axis))
+    grown, reach = (shard, 1)
+    while reach < ways:
+        theirs = lax.ppermute(grown, axis, [(d, d ^ reach) for d in range(ways)])
+        mine_first = jnp.concatenate([grown, theirs], axis=dim)
+        theirs_first = jnp.concatenate([theirs, grown], axis=dim)
+        grown = jnp.where(here & reach == 0, mine_first, theirs_first)
+        reach = 2 * reach
+    return grown
 
 
 def spread(block, axis, holder):
@@ -71,7 +83,7 @@
     swept_half = swept_factor.astype(jnp.bfloat16)
     partial_terms = lax.dot_general(
         swept_half,
-        lax.all_gather(gradients, "shard", axis=0, tiled=True),
+        doubled_up(gradients, "shard", 0),
         (((1,), (1,)), ((), ())),
         preferred_element_type=jnp.float32,
     )

time: 592 us -> 914 us (1.54)
  waiting for transfers between devices: 423 us -> 643 us
  blocking collectives: 24.8 us -> 106 us
  other arithmetic: 69.1 us -> 82.9 us
    psum x4, waiting for transfers between devices: 243 us -> 542 us  [spread(): return lax.psum(block, axis)]
    all_gather x1 -> x0, waiting for transfers between devices: 127 us -> none  [on_device(): lax.all_gather(gradients, 'shard', axis=0, tiled=True)]
    all_gather x1, blocking collectives: 24.8 us -> 106 us  [on_device(): token_piece = lax.all_gather(samples, 'shard', axis=0, tiled=True)]
    ppermute x0 -> x4, waiting for transfers between devices: none -> 48.5 us  [doubled_up(): theirs = lax.ppermute(grown, axis, [(d, d ^ reach) for d in range(ways)])]
    select_n x0 -> x3, other arithmetic: none -> 19.3 us  [doubled_up(): grown = jnp.where(here & reach == 0, mine_first, theirs_first)]
  transfers between devices with their start and end apart: 6 -> 9, of which waited for: 6 -> 7; matrix products, arithmetic and copies ran while one was open for 1% -> 10% of each run, Pallas kernels for 0% -> 0%
where the time goes in v1:
time: 914 us; the launch traced here: 913 us
  waiting for transfers between devices  643 us (70%)
  blocking collectives  106 us (12%)
  other arithmetic  82.9 us (9%)
  matrix products  50.6 us (6%)
  between operations  15.9 us (2%)
    psum x4, waiting for transfers between devices, spread(): return lax.psum(block, axis)  542 us
    all_gather x1, blocking collectives, on_device(): token_piece = lax.all_gather(samples, 'shard', axis=0, tiled=True)  106 us
    reduce_scatter x1, waiting for transfers between devices, on_device(): lax.psum_scatter(partial_terms, 'group', scatter_dimension=1, tiled=True)  53.1 us
    ppermute x4, waiting for transfers between devices, doubled_up(): theirs = lax.ppermute(grown, axis, [(d, d ^ reach) for d in range(ways)])  48.5 us
    another operation x6, other arithmetic, solve_spd(): lower_factor = jnp.linalg.cholesky(pivot_block)  24.8 us
    another operation x4, other arithmetic, solve_spd(): lax.linalg.triangular_solve(lower_factor, half_solved, left_side=True, lo...  20.9 us
    select_n x3, other arithmetic, doubled_up(): grown = jnp.where(here & reach == 0, mine_first, theirs_first)  19.3 us
  transfers between devices with their start and end apart: 9, of which 7 were waited for; matrix products, arithmetic and copies ran while one was open for 10% of the time, Pallas kernels for 0%

profile of v1, /device:TPU:0, one launch (start us, length us, event | category | flops | bytes accessed | tf_op | source)
XLA Modules:
  0.0 913.4 jit_solution(1676411638051019)
XLA Ops:
  16.3 46.0 %collective-permute-done.1 = bf16[256,4096]{1,0:T(8,128)(2,1)} collective-permute-done((bf16[256,4096]{1,0:T(8,128)(2,1)S(1)}, bf16[256,4096]{1,0:T(8,128)(2,1)}, u32[]{:S(2)}, u32[]{:S(2)}) %collective-permute-start.1) | collective-permute-done | bytes 2097184 | tf_op jit(solution)/shard_map/ppermute | solution.py:16
  62.3 4.7 maximum_select_fusion.3
  69.4 106.1 %all-gather = bf16[16,2,8192]{2,1,0:T(2,128)(2,1)S(1)} all-gather(bf16[1,2,8192]{2,1,0:T(2,128)(2,1)S(1)} %bitcast.33), channel_id=1, replica_groups=mesh['group'=2,'shard'=16] {'shard'}, dimensions={0}, use_global_device_ids=true | all-gather | bytes 557056 | tf_op jit(solution)/shard_map/all_gather | solution.py:45
  175.8 12.4 %maximum_select_fusion.2 = bf16[1024,4096]{1,0:T(8,128)(2,1)} fusion(bf16[512,4096]{1,0:T(8,128)(2,1)} %collective-permute-done.2, bf16[512,4096]{1,0:T(8,128)(2,1)} %maximum_select_fusion.3, pred[]{:T(512)S(6)} %eq.62), kind=kLoop, calls=%fused_computation.37 | loop fusion | flops 37748736 | bytes 16777216 | tf_op jit(solution)/shard_map/jit(_where)/select_n | solution.py:19
  188.2 4.6 select_add_fusion
  192.8 639.5 %while.17 = (s32[]{:T(128)}, f32[512,4096]{1,0:T(8,128)}, s32[]{:T(128)}, s32[4096]{0:T(1024)S(1)}, s32[]{:T(128)}, /*index=5*/s32[]{:T(128)}, s32[]{:T(128)}, s...) while((s32[]{:T(128)}, f32[512,4096]{1,0:T(8,128)}, ...), condition=%wide.region_6.7_spmd.clone, body=%wide.region_0.6_spmd.clone.sunk | while | flops 4838440960 | bytes 122046224 | solution.py:82
  194.6 3.1 dynamic-slice_select_fusion.7
  197.7 21.7 %all-reduce.6.cloned.1.call-done = f32[512,128]{1,0:T(8,128)} async-done(((f32[512,128]{1,0:T(8,128)}), f32[512,128]{1,0:T(8,128)}) %all-reduce.6.cloned.1.call-update) | async-done | bytes 262160 | tf_op jit(solution)/shard_map/while/body/eval_jaxpr/psum | solution.py:26
  221.0 397.9 %all-reduce.8.cloned.1.call-done = (f32[128,4096]{1,0:T(8,128)}, f32[128,128]{1,0:T(8,128)}) async-done(((f32[128,4096]{1,0:T(8,128)}, f32[128,128]{1,0:T(8,128)}), (f32[128,4096]{1,0:T(8,128)}, f32[128,128]{1,0:T(8,128)})) %all-reduce.8.cloned.1.call-update) | async-done | bytes 2162704 | tf_op jit(solution)/shard_map/while/body/eval_jaxpr/psum | solution.py:26
  620.7 11.7 %cholesky.59 = f32[128,128]{1,0:T(8,128)S(1)} custom-call(f32[128,128]{1,0:T(8,128)S(1)} %fusion.51), custom_call_target="Cholesky" | custom-call | tf_op jit(solution)/shard_map/while/body/eval_jaxpr/jit(cholesky)/cholesky | solution.py:30
  633.7 9.8 %custom-call.26 = f32[1,128,128]{1,2,0:T(8,128)S(1)} custom-call(f32[1,128,128]{2,1,0:T(8,128)S(1)} %fusion.52), custom_call_target="InvertDiagBlocksLowerTriangular" | custom-call | tf_op jit(solution)/shard_map/while/body/eval_jaxpr/triangular_solve | solution.py:32
  643.6 3.7 fusion.53
  649.2 8.3 convolution_subtract_fusion.2
  657.9 3.4 copy-done.1
  663.1 3.1 dynamic-slice_select_fusion.7
  666.2 20.7 %all-reduce.6.cloned.1.call-done = f32[512,128]{1,0:T(8,128)} async-done(((f32[512,128]{1,0:T(8,128)}), f32[512,128]{1,0:T(8,128)}) %all-reduce.6.cloned.1.call-update) | async-done | bytes 262160 | tf_op jit(solution)/shard_map/while/body/eval_jaxpr/psum | solution.py:26
  688.5 101.3 %all-reduce.8.cloned.1.call-done = (f32[128,4096]{1,0:T(8,128)}, f32[128,128]{1,0:T(8,128)}) async-done(((f32[128,4096]{1,0:T(8,128)}, f32[128,128]{1,0:T(8,128)}), (f32[128,4096]{1,0:T(8,128)}, f32[128,128]{1,0:T(8,128)})) %all-reduce.8.cloned.1.call-update) | async-done | bytes 2162704 | tf_op jit(solution)/shard_map/while/body/eval_jaxpr/psum | solution.py:26
  791.6 11.7 %cholesky.59 = f32[128,128]{1,0:T(8,128)S(1)} custom-call(f32[128,128]{1,0:T(8,128)S(1)} %fusion.51), custom_call_target="Cholesky" | custom-call | tf_op jit(solution)/shard_map/while/body/eval_jaxpr/jit(cholesky)/cholesky | solution.py:30
  804.7 9.8 %custom-call.26 = f32[1,128,128]{1,2,0:T(8,128)S(1)} custom-call(f32[1,128,128]{2,1,0:T(8,128)S(1)} %fusion.52), custom_call_target="InvertDiagBlocksLowerTriangular" | custom-call | tf_op jit(solution)/shard_map/while/body/eval_jaxpr/triangular_solve | solution.py:32
  814.5 3.7 fusion.53
  820.2 8.3 convolution_subtract_fusion.2
  828.9 3.4 copy-done.1
  832.3 18.2 %fusion.20 = f32[512,2048]{1,0:T(8,128)} fusion(bf16[1024,4096]{1,0:T(8,128)(2,1)} %collective-permute-done.3, bf16[1024,4096]{1,0:T(8,128)(2,1)} %maximum_select_fusion.2, pred[]{:T(512)S(6)} %eq.61, f32[512,4096]{1,0:T(8,128)} %get-tuple-element.154), kind=kOutput, calls=%fused_computation.30 | convolution fusion | flops 8667529216 | bytes 29360128 | tf_op jit(solution)/shard_map/dot_general | solution.py:84
  850.5 53.1 %reduce-scatter.2.cloned.1.call-done = f32[512,1024]{1,0:T(8,128)} async-done(((f32[512,2048]{1,0:T(8,128)}), f32[512,1024]{1,0:T(8,128)}) %reduce-scatter.2.cloned.1.call-update) | async-done | bytes 2097168 | tf_op jit(solution)/shard_map/reduce_scatter | solution.py:90
  (57 shorter events, 30.5 us)
Async XLA Ops:
  8.0 61.4 %copy-start.3 = (bf16[2,8192]{1,0:T(2,128)(2,1)S(1)}, bf16[2,8192]{1,0:T(2,128)(2,1)}, u32[]{:S(2)}) copy-start(bf16[2,8192]{1,0:T(2,128)(2,1)} %param.6) | copy-start | bytes 98308
  8.0 3.1 collective-permute-start
  13.3 49.0 %collective-permute-start.1 = (bf16[256,4096]{1,0:T(8,128)(2,1)S(1)}, bf16[256,4096]{1,0:T(8,128)(2,1)}, u32[]{:S(2)}, u32[]{:S(2)}) collective-permute-start(bf16[256,4096]{1,0:T(8,128)(2,1)S(1)} %maximum_select_fusion.4), channel_id=1, source_target_pairs={{0,2},{1,3},{2,0},{3,1},{4,6},{5,7},{6,4},{7,5},{8,10},{9,11},{10,... | collective-permute-start | bytes 6291464 | tf_op jit(solution)/shard_map/ppermute | solution.py:16
  67.0 108.8 %collective-permute-start.2 = (bf16[512,4096]{1,0:T(8,128)(2,1)}, bf16[512,4096]{1,0:T(8,128)(2,1)}, u32[]{:S(2)}, u32[]{:S(2)}) collective-permute-start(bf16[512,4096]{1,0:T(8,128)(2,1)} %maximum_select_fusion.3), channel_id=1, source_target_pairs={{0,4},{1,5},{2,6},{3,7},{4,0},{5,1},{6,2},{7,3},{8,12},{9,13},{10,... | collective-permute-start | bytes 12582920 | tf_op jit(solution)/shard_map/ppermute | solution.py:16
  175.7 12.4 %slice-start = ((s8[8388608]{0:T(1024)(128)(4,1)}), s8[4194304]{0:T(1024)(128)(4,1)S(1)}, s32[]{:S(2)}) async-start(s8[8388608]{0:T(1024)(128)(4,1)} %bitcast.31), calls=%async_computation.4 | async-start | bytes 8388608
  175.7 12.4 %slice-start.1 = ((s8[8388608]{0:T(1024)(128)(4,1)}), s8[4194304]{0:T(1024)(128)(4,1)S(1)}, s32[]{:S(2)}) async-start(s8[8388608]{0:T(1024)(128)(4,1)} %bitcast.31), calls=%async_computation.5 | async-start | bytes 8388608
  188.2 644.1 %collective-permute-start.3 = (bf16[1024,4096]{1,0:T(8,128)(2,1)}, bf16[1024,4096]{1,0:T(8,128)(2,1)}, u32[]{:S(2)}, u32[]{:S(2)}) collective-permute-start(bf16[1024,4096]{1,0:T(8,128)(2,1)} %maximum_select_fusion.2), channel_id=1, source_target_pairs={{0,8},{1,9},{2,10},{3,11},{4,12},{5,13},{6,14},{7,15},{8,0},{9,1},... | collective-permute-start | bytes 25165832 | tf_op jit(solution)/shard_map/ppermute | solution.py:16
  192.8 26.6 %all-reduce.6.cloned.1.call-start = ((), (), s32[]{:S(2)}) async-start(), calls=%async_computation.2 | async-start | bytes 524288 | tf_op jit(solution)/shard_map/while/body/eval_jaxpr/psum | solution.py:26
  194.5 424.4 %all-reduce.8.cloned.1.call-start = ((), (), s32[]{:S(2)}) async-start(), calls=%async_computation.3 | async-start | bytes 4325376 | tf_op jit(solution)/shard_map/while/body/eval_jaxpr/psum | solution.py:26
  219.4 429.8 %copy-start.2 = (f32[512,128]{1,0:T(8,128)S(1)}, f32[512,128]{1,0:T(8,128)}, u32[]{:S(2)}) copy-start(f32[512,128]{1,0:T(8,128)} %all-reduce.6.cloned.1.call-done) | copy-start | bytes 786436 | tf_op jit(solution)/shard_map/while
  643.6 5.7 copy-start
  657.9 3.4 copy-start.1
  661.3 25.6 %all-reduce.6.cloned.1.call-start = ((), (), s32[]{:S(2)}) async-start(), calls=%async_computation.2 | async-start | bytes 524288 | tf_op jit(solution)/shard_map/while/body/eval_jaxpr/psum | solution.py:26
  663.0 126.8 %all-reduce.8.cloned.1.call-start = ((), (), s32[]{:S(2)}) async-start(), calls=%async_computation.3 | async-start | bytes 4325376 | tf_op jit(solution)/shard_map/while/body/eval_jaxpr/psum | solution.py:26
  687.0 133.2 %copy-start.2 = (f32[512,128]{1,0:T(8,128)S(1)}, f32[512,128]{1,0:T(8,128)}, u32[]{:S(2)}) copy-start(f32[512,128]{1,0:T(8,128)} %all-reduce.6.cloned.1.call-done) | copy-start | bytes 786436 | tf_op jit(solution)/shard_map/while
  814.5 5.7 copy-start
  828.9 3.4 copy-start.1
  832.3 71.3 %reduce-scatter.2.cloned.1.call-start = ((), (), s32[]{:S(2)}) async-start(), calls=%async_computation.1 | async-start | bytes 6291456 | tf_op jit(solution)/shard_map/reduce_scatter | solution.py:90
Sparse Core Ops, SparseCore 0:
  196.4 22.9 all-reduce.5
  223.6 395.2 all-reduce.7
  665.0 21.9 all-reduce.5
  691.0 98.8 all-reduce.7
Sparse Core Ops, SparseCore 1:
  850.6 53.0 reduce-scatter.1
